TPU v7x, 32 devices: a whole 2x2x4 slice. The times are simulated.
32 devices in a mesh: dp: 8 (over z, core), mp: 4 (over y, x).
Axes of the slice: x: 2, y: 2, z: 4, core: 2. Of those that a mesh axis runs over, the one named last changes fastest.
Arguments:
- x_in: bfloat16 [8, 1024, 2048], P('dp'), may hold values from -6 to 6
- lengths: int32 [8], P('dp'), may hold values from 512 to 1024, as said below
- gain_attn: bfloat16 [2048], P('dp'), may hold values from 0.5 to 1.5
- query_weight: bfloat16 [2048, 2048], P('dp', 'mp'), may hold values from -0.125 to 0.125
- key_projection_matrix: bfloat16 [2048, 4, 256], P('dp', None, 'mp'), may hold values from -0.125 to 0.125
- value_projection_matrix: bfloat16 [2048, 4, 256], P('dp', None, 'mp'), may hold values from -0.125 to 0.125
- out_weight: bfloat16 [2048, 2048], P('mp', 'dp'), may hold values from -0.75 to 0.75
- gain_ffn: bfloat16 [2048], P('dp'), may hold values from 0.5 to 1.5
- gate_weight: bfloat16 [2048, 8192], P('dp', 'mp'), may hold values from -0.125 to 0.125
- up_weight: bfloat16 [2048, 8192], P('dp', 'mp'), may hold values from -0.125 to 0.125
- down_weight: bfloat16 [8192, 2048], P('mp', 'dp'), may hold values from -0.0625 to 0.0625
- cotangent: bfloat16 [8, 1024, 2048], P('dp'), may hold values from -6 to 6
Outputs:
- layer_out: bfloat16 [8, 1024, 2048], P('dp')
- grad_input: float32 [8, 1024, 2048], P('dp')
- gain_attn_grad: float32 [2048], P('dp')
- query_grad: float32 [2048, 2048], P('dp', 'mp')
- key_projection_grad: float32 [2048, 4, 256], P('dp', None, 'mp')
- value_projection_grad: float32 [2048, 4, 256], P('dp', None, 'mp')
- out_grad: float32 [2048, 2048], P('mp', 'dp')
- gain_ffn_grad: float32 [2048], P('dp')
- gate_grad: float32 [2048, 8192], P('dp', 'mp')
- up_grad: float32 [2048, 8192], P('dp', 'mp')
- down_grad: float32 [8192, 2048], P('mp', 'dp')
Inputs may be any that keep to these rules, and one draw needn't show every extreme that they name: A sequence's valid slots are its first lengths positions; in every draw some sequence fills all 1024 slots.
All inputs are finite; a program needn't handle non-finite values.
Results may differ from a plain program's by a relative error of at most 0.014.
Values may be sent and summed in bfloat16 or wider, within the bound.
No kernel may reach another device: no remote copies, remote signals or barrier semaphores. Data moves between devices by JAX's collectives and lax.ppermute only.
A program may use at most 256 MiB of HBM per device.

v0:
```python
import jax
import jax.numpy as jnp
from jax import lax
from jax.sharding import PartitionSpec as P

QUERY_HEADS = 8
KEY_VALUE_HEADS = 4
HEAD_SIZE = 256
eps_norm = 1e-06
rope_base = 1000042.0
neg_large = -1e30
bf16 = jnp.bfloat16
f32 = jnp.float32


def rope_tables(slot_length, size):
    half_size = size // 2
    inv_freq = rope_base ** (-(jnp.arange(half_size, dtype=f32) * 2.0 / size))
    angles = jnp.arange(slot_length, dtype=f32)[:, None] * inv_freq[None, :]
    return (jnp.cos(angles), jnp.sin(angles))


def rotate(values, cos_b, sin_b):
    half = values.shape[-1] // 2
    a, b = (values[..., :half], values[..., half:])
    return jnp.concatenate([a * cos_b - b * sin_b, b * cos_b + a * sin_b], axis=-1)


def rotate_back(grads, cos_b, sin_b):
    half = grads.shape[-1] // 2
    a, b = (grads[..., :half], grads[..., half:])
    return jnp.concatenate([a * cos_b + b * sin_b, b * cos_b - a * sin_b], axis=-1)


def mm(left, right):
    return lax.dot_general(left, right, (((1,), (0,)), ((), ())), preferred_element_type=f32)


def mm_t(left, right):
    return lax.dot_general(left, right, (((1,), (1,)), ((), ())), preferred_element_type=f32)


def mm_rows(left, right):
    return lax.dot_general(left, right, (((0,), (0,)), ((), ())), preferred_element_type=f32)


OVER_X = [(0, 1), (1, 0), (2, 3), (3, 2)]
OVER_Y = [(0, 2), (2, 0), (1, 3), (3, 1)]


def pick(blocks, which):
    return lax.dynamic_index_in_dim(blocks, which, 0, keepdims=False)


def scatter_rows(product, lefts, width):
    mp_size = lax.axis_size("mp")
    rows = lefts[0].shape[0]
    here = rows // mp_size
    if mp_size != 4:
        part = jnp.concatenate([product(lefts, 0), product(lefts, 1)], axis=1).astype(bf16)
        return lax.psum_scatter(part, "mp", scatter_dimension=0, tiled=True).astype(f32)
    me = lax.axis_index("mp")
    x, y = (me % 2, me // 2)
    half = width // 2

    def rows_x(which):
        return [
            lax.dynamic_index_in_dim(
                v.reshape(2, 2, here, v.shape[1]), which, 1, keepdims=False
            ).reshape(2 * here, v.shape[1])
            for v in lefts
        ]

    def rows_y(which):
        return [
            lax.dynamic_index_in_dim(v.reshape(2, 2 * here, v.shape[1]), which, 0, keepdims=False)
            for v in lefts
        ]

    away_a = lax.ppermute(product(rows_x(1 - x), 0).astype(bf16), "mp", OVER_X)
    away_b = lax.ppermute(product(rows_y(1 - y), 1).astype(bf16), "mp", OVER_Y)
    sum_a = (product(rows_x(x), 0) + away_a.astype(f32)).reshape(2, here, half)
    sum_b = (product(rows_y(y), 1) + away_b.astype(f32)).reshape(2, here, half)
    last_a = lax.ppermute(pick(sum_a, 1 - y).astype(bf16), "mp", OVER_Y)
    last_b = lax.ppermute(pick(sum_b, 1 - x).astype(bf16), "mp", OVER_X)
    return jnp.concatenate(
        [pick(sum_a, y) + last_a.astype(f32), pick(sum_b, x) + last_b.astype(f32)], axis=1
    )


def gather_rows(block):
    mp_size = lax.axis_size("mp")
    if mp_size != 4:
        return lax.all_gather(block, "mp", axis=0, tiled=True)
    me = lax.axis_index("mp")
    x, y = (me % 2, me // 2)
    here, width = block.shape
    half = width // 2
    own_a, own_b = (block[:, :half], block[:, half:])

    def both(own, other, low):
        return (jnp.where(low, own, other), jnp.where(low, other, own))

    got_a = lax.ppermute(own_a, "mp", OVER_Y)
    got_b = lax.ppermute(own_b, "mp", OVER_X)
    pair_a = jnp.stack(both(own_a, got_a, y == 0))
    pair_b = jnp.stack(both(own_b, got_b, x == 0))
    far_a = lax.ppermute(pair_a, "mp", OVER_X)
    far_b = lax.ppermute(pair_b, "mp", OVER_Y)
    all_a = jnp.stack(both(pair_a, far_a, x == 0), axis=1)
    all_b = jnp.stack(both(pair_b, far_b, y == 0), axis=0)
    return jnp.concatenate([all_a.reshape(4 * here, half), all_b.reshape(4 * here, half)], axis=1)


def mask_block(first_row, block_rows, slots, seq_len):
    q_pos = first_row + jnp.arange(block_rows)
    k_pos = jnp.arange(slots)
    return (k_pos[None, :] <= q_pos[:, None]) & (k_pos[None, :] < seq_len)


def attend(queries, keys, values, seq_len, factor):
    slots = keys.shape[0]
    block_rows = min(512, slots)
    parts, totals = ([], [])
    for first_row in range(0, slots, block_rows):
        upto = first_row + block_rows
        raw = jnp.einsum(
            "qhd,kd->hqk", queries[first_row:upto], keys[:upto], preferred_element_type=f32
        )
        allowed = mask_block(first_row, block_rows, upto, seq_len)
        scores = jnp.where(allowed[None], raw * factor, neg_large)
        row_max = jnp.max(scores, axis=-1, keepdims=True)
        exps = jnp.exp(scores - row_max)
        total = jnp.sum(exps, axis=-1, keepdims=True)
        probs = (exps / total).astype(bf16)
        parts.append(
            jnp.einsum("hqk,kd->qhd", probs, values[:upto], preferred_element_type=f32).astype(bf16)
        )
        totals.append((row_max + jnp.log(total))[..., 0])
    return (jnp.concatenate(parts, axis=0), jnp.concatenate(totals, axis=1))


def attend_back(queries, keys, values, grad_ctx, log_total, seq_len, factor):
    slots = keys.shape[0]
    block_rows = min(512, slots)
    dq_parts = []
    d_keys = jnp.zeros(keys.shape, f32)
    d_values = jnp.zeros(values.shape, f32)
    for first_row in range(0, slots, block_rows):
        upto = first_row + block_rows
        q_block = queries[first_row:upto]
        g_block = grad_ctx[first_row:upto]
        raw = jnp.einsum("qhd,kd->hqk", q_block, keys[:upto], preferred_element_type=f32)
        allowed = mask_block(first_row, block_rows, upto, seq_len)
        scores = jnp.where(allowed[None], raw * factor, neg_large)
        probs = jnp.exp(scores - log_total[:, first_row:upto, None])
        grad_p = jnp.einsum("qhd,kd->hqk", g_block, values[:upto], preferred_element_type=f32)
        inner = jnp.sum(probs * grad_p, axis=-1, keepdims=True)
        grad_s = (probs * (grad_p - inner) * factor).astype(bf16)
        dq_parts.append(jnp.einsum("hqk,kd->qhd", grad_s, keys[:upto], preferred_element_type=f32))
        dk = jnp.einsum("hqk,qhd->kd", grad_s, q_block, preferred_element_type=f32)
        dv = jnp.einsum("hqk,qhd->kd", probs.astype(bf16), g_block, preferred_element_type=f32)
        d_keys = d_keys.at[:upto].add(dk)
        d_values = d_values.at[:upto].add(dv)
    return (jnp.concatenate(dq_parts, axis=0), d_keys, d_values)


def spread_heads(block):
    mp_size = lax.axis_size("mp")
    rows, heads, part = block.shape
    send = jnp.repeat(block, mp_size // heads, axis=1)
    got = lax.all_to_all(send, "mp", 1, 1, tiled=True)
    return got.reshape(rows, mp_size * part)


def collect_heads(block, heads):
    mp_size = lax.axis_size("mp")
    rows, size = block.shape
    got = lax.all_to_all(block.reshape(rows, mp_size, size // mp_size), "mp", 1, 1, tiled=True)
    got = got.reshape(rows, heads, mp_size // heads, size // mp_size)
    return jnp.sum(got.astype(f32), axis=2)


def gather_dp(block):
    return lax.all_gather(block, "dp", axis=0, tiled=True)


def reduce_dp(block):
    return lax.psum_scatter(block, "dp", scatter_dimension=0, tiled=True)


def local(
    x_in,
    lengths,
    gain_attn,
    query_weight,
    key_projection_matrix,
    value_projection_matrix,
    out_weight,
    gain_ffn,
    gate_weight,
    up_weight,
    down_weight,
    cotangent,
):
    _, slots, width = x_in.shape
    mp_size = lax.axis_size("mp")
    me = lax.axis_index("mp")
    heads_here = query_weight.shape[1] // HEAD_SIZE
    q_cols = query_weight.shape[1]
    factor = HEAD_SIZE ** (-0.5)
    here = slots // mp_size
    seq_len = lengths[0]
    cos_t, sin_t = rope_tables(slots, HEAD_SIZE)
    kv_block = jnp.concatenate(
        [spread_heads(key_projection_matrix), spread_heads(value_projection_matrix)], axis=1
    )
    gains = lax.all_gather(jnp.stack([gain_attn, gain_ffn]), "dp", axis=1, tiled=True).astype(f32)
    g_attn, g_ffn = (gains[0], gains[1])
    w_q = gather_dp(query_weight)
    w_kv = gather_dp(kv_block)
    w_o = gather_dp(out_weight.T)
    w_g = gather_dp(gate_weight)
    w_u = gather_dp(up_weight)
    w_d = gather_dp(down_weight.T)
    tok = x_in[0].astype(f32)
    r1 = lax.rsqrt(jnp.mean(tok * tok, axis=-1, keepdims=True) + eps_norm)
    h_attn = (tok * r1 * g_attn).astype(bf16)
    cos_h, sin_h = (cos_t[:, None, :], sin_t[:, None, :])
    queries = rotate(mm(h_attn, w_q).reshape(slots, heads_here, HEAD_SIZE), cos_h, sin_h).astype(
        bf16
    )
    kv_lin = mm(h_attn, w_kv)
    keys = rotate(kv_lin[:, :HEAD_SIZE], cos_t, sin_t).astype(bf16)
    values = kv_lin[:, HEAD_SIZE:].astype(bf16)
    context, log_total = attend(queries, keys, values, seq_len, factor)
    context = context.reshape(slots, q_cols)
    half = width // 2

    def product_out(lefts, which):
        return mm_t(lefts[0], w_o[which * half : (which + 1) * half])

    attn_rows = scatter_rows(product_out, [context], width)
    tok_here = lax.dynamic_slice_in_dim(x_in[0], me * here, here, 0).astype(f32)
    mid = tok_here + attn_rows
    r2 = lax.rsqrt(jnp.mean(mid * mid, axis=-1, keepdims=True) + eps_norm)
    n2 = mid * r2
    h_ffn = gather_rows((n2 * g_ffn).astype(bf16))
    gate = mm(h_ffn, w_g)
    up = mm(h_ffn, w_u)
    sig = jax.nn.sigmoid(gate)
    hidden = (gate * sig * up).astype(bf16)
    valid = (jnp.arange(slots)[:, None] < seq_len).astype(bf16)
    grad_low = cotangent[0] * valid
    down_grad = mm_rows(grad_low, hidden).astype(bf16)
    down_out = reduce_dp(down_grad)
    d_hidden = mm(grad_low, w_d)
    d_gate = (d_hidden * up * sig * (1.0 + gate * (1.0 - sig))).astype(bf16)
    d_up = (d_hidden * gate * sig).astype(bf16)

    def product_h2(lefts, which):
        cols = slice(which * half, (which + 1) * half)
        return mm_t(lefts[0], w_g[cols]) + mm_t(lefts[1], w_u[cols])

    d_h2 = scatter_rows(product_h2, [d_gate, d_up], width)
    gate_out = reduce_dp(mm_rows(h_ffn, d_gate).astype(bf16))
    up_out = reduce_dp(mm_rows(h_ffn, d_up).astype(bf16))
    gain_ffn_part = jnp.sum(d_h2 * n2, axis=0)
    e2 = d_h2 * g_ffn
    grad_here = lax.dynamic_slice_in_dim(grad_low, me * here, here, 0).astype(f32)
    g1 = grad_here + r2 * (e2 - n2 * jnp.mean(e2 * n2, axis=-1, keepdims=True))
    g1_low = gather_rows(g1.astype(bf16))

    def product_ffn(lefts, which):
        return mm_t(lefts[0], w_d[which * half : (which + 1) * half])

    ffn_rows = scatter_rows(product_ffn, [hidden], width)
    layer_out = gather_rows((mid + ffn_rows).astype(bf16))
    d_context = mm(g1_low, w_o).astype(bf16).reshape(slots, heads_here, HEAD_SIZE)
    out_out = reduce_dp(mm_rows(g1_low, context).astype(bf16))
    dq, dk, dv = attend_back(queries, keys, values, d_context, log_total, seq_len, factor)
    d_q = rotate_back(dq, cos_h, sin_h).astype(bf16).reshape(slots, q_cols)
    d_kv = jnp.concatenate([rotate_back(dk, cos_t, sin_t), dv], axis=1).astype(bf16)
    q_out = reduce_dp(mm_rows(h_attn, d_q).astype(bf16))
    kv_out = reduce_dp(mm_rows(h_attn, d_kv).astype(bf16))

    def product_h1(lefts, which):
        cols = slice(which * half, (which + 1) * half)
        return mm_t(lefts[0], w_q[cols]) + mm_t(lefts[1], w_kv[cols])

    d_h1 = scatter_rows(product_h1, [d_q, d_kv], width)
    r1_here = lax.dynamic_slice_in_dim(r1, me * here, here, 0)
    n1 = tok_here * r1_here
    gain_attn_part = jnp.sum(d_h1 * n1, axis=0)
    e1 = d_h1 * g_attn
    grad_in = g1 + r1_here * (e1 - n1 * jnp.mean(e1 * n1, axis=-1, keepdims=True))
    grad_input = gather_rows(grad_in.astype(bf16)).astype(f32)
    gain_parts = lax.psum(jnp.stack([gain_attn_part, gain_ffn_part]), ("dp", "mp"))
    rows_here = gain_attn.shape[0]
    gain_grads = lax.dynamic_slice_in_dim(
        gain_parts, lax.axis_index("dp") * rows_here, rows_here, 1
    )
    key_grad = collect_heads(kv_out[:, :HEAD_SIZE], KEY_VALUE_HEADS)
    value_grad = collect_heads(kv_out[:, HEAD_SIZE:], KEY_VALUE_HEADS)
    return (
        layer_out[None],
        grad_input[None],
        gain_grads[0],
        q_out.astype(f32),
        key_grad,
        value_grad,
        out_out.T.astype(f32),
        gain_grads[1],
        gate_out.astype(f32),
        up_out.astype(f32),
        down_out.T.astype(f32),
    )


def solution(mesh):
    return jax.shard_map(
        local,
        mesh=mesh,
        in_specs=(
            P("dp", None, None),
            P("dp"),
            P("dp"),
            P("dp", "mp"),
            P("dp", None, "mp"),
            P("dp", None, "mp"),
            P("mp", "dp"),
            P("dp"),
            P("dp", "mp"),
            P("dp", "mp"),
            P("mp", "dp"),
            P("dp", None, None),
        ),
        out_specs=(
            P("dp", None, None),
            P("dp", None, None),
            P("dp"),
            P("dp", "mp"),
            P("dp", None, "mp"),
            P("dp", None, "mp"),
            P("mp", "dp"),
            P("dp"),
            P("dp", "mp"),
            P("dp", "mp"),
            P("mp", "dp"),
        ),
        check_vma=False,
    )
```

profile of v0, /device:TPU:0, one launch (start us, length us, event | category | flops | bytes accessed | tf_op | source)
XLA Modules:
  0.0 940.7 jit_solution(466775596118007731)
XLA Ops:
  8.0 10.2 %all_to_all.20 = bf16[256,4,64]{0,2,1:T(8,128)(2,1)S(1)} all-to-all(bf16[256,4,64]{0,2,1:T(8,128)(2,1)} %param.28), channel_id=1, replica_groups=mesh['dp'=8,'mp'=4] {'mp'}, dimensions={1} | all-to-all | bytes 262144 | tf_op jit(solution)/shard_map/all_to_all | solution.py:172
  33.7 12.0 %all_gather.21 = bf16[2,2048]{1,0:T(2,128)(2,1)S(1)} all-gather(bf16[2,256]{1,0:T(2,128)(2,1)S(1)} %pad_maximum_fusion.34), channel_id=1, replica_groups=mesh['dp'=8,'mp'=4] {'dp'}, dimensions={1}, use_global_device_ids=true | all-gather | bytes 9216 | tf_op jit(solution)/shard_map/all_gather | solution.py:218
  56.1 17.9 %all-gather.7.cloned.1.call-done = bf16[2048,512]{0,1:T(8,128)(2,1)} async-done(((bf16[256,512]{0,1:T(8,128)(2,1)}), bf16[2048,512]{0,1:T(8,128)(2,1)}) %all-gather.7.cloned.1.call-update) | async-done | bytes 2097168 | tf_op jit(solution)/shard_map/all_gather | solution.py:185
  94.3 11.2 %all-gather.11.cloned.1.call-done = bf16[2048,512]{0,1:T(8,128)(2,1)} async-done(((bf16[256,512]{0,1:T(8,128)(2,1)}), bf16[2048,512]{0,1:T(8,128)(2,1)}) %all-gather.11.cloned.1.call-update) | async-done | bytes 2097168 | tf_op jit(solution)/shard_map/all_gather | solution.py:185
  125.0 9.1 collective-permute-done.2
  167.0 9.1 collective-permute-done.4
  183.6 16.3 %collective-permute-done.7 = bf16[2,256,1024]{2,1,0:T(8,128)(2,1)S(1)} collective-permute-done((bf16[2,256,1024]{2,1,0:T(8,128)(2,1)S(1)}, bf16[2,256,1024]{2,1,0:T(8,128)(2,1)S(1)}, u32[]{:S(2)}, u32[]{:S(2)}) %collective-permute-start.7) | collective-permute-done | bytes 1048608 | tf_op jit(solution)/shard_map/ppermute | solution.py:109
  203.2 14.8 %fusion.237 = f32[1024,2048]{1,0:T(8,128)} fusion(bf16[1024,2048]{1,0:T(8,128)(2,1)} %bitcast_multiply_fusion.1, bf16[2048,2048]{0,1:T(8,128)(2,1)} %all-gather.17.cloned.1.call-done), kind=kOutput, calls=%fused_computation.365 | convolution fusion | flops 8589934592 | bytes 20971520 | tf_op jit(solution)/shard_map/dot_general | solution.py:36
  218.0 52.4 %all-gather.15.cloned.1.call-done = bf16[2048,2048]{1,0:T(8,128)(2,1)} async-done(((bf16[256,2048]{1,0:T(8,128)(2,1)}), bf16[2048,2048]{1,0:T(8,128)(2,1)}) %all-gather.15.cloned.1.call-update) | async-done | bytes 8388624 | tf_op jit(solution)/shard_map/all_gather | solution.py:185
  270.3 14.4 %fusion.223 = f32[1024,2048]{1,0:T(8,128)} fusion(bf16[2048,2048]{1,0:T(8,128)(2,1)} %all-gather.15.cloned.1.call-done, bf16[1024,1024]{1,0:T(8,128)(2,1)} %bitcast.429, bf16[1024,1024]{1,0:T(8,128)(2,1)} %bitcast.433), kind=kOutput, calls=%fused_computation.351 | convolution fusion | flops 8598323200 | bytes 20971520 | tf_op jit(solution)/shard_map/dot_general | solution.py:36
  284.8 67.6 %all-gather.13.cloned.1.call-done = bf16[2048,2048]{1,0:T(8,128)(2,1)} async-done(((bf16[256,2048]{1,0:T(8,128)(2,1)}), bf16[2048,2048]{1,0:T(8,128)(2,1)}) %all-gather.13.cloned.1.call-update) | async-done | bytes 8388624 | tf_op jit(solution)/shard_map/all_gather | solution.py:185
  352.4 21.8 %multiply_convert_fusion.1 = (bf16[1024,2048]{1,0:T(8,128)(2,1)}, bf16[1024,2048]{1,0:T(8,128)(2,1)}, bf16[1024,2048]{1,0:T(8,128)(2,1)}) fusion(f32[1024,2048]{1,0:T(8,128)} %fusion.237, f32[1024,2048]{1,0:T(8,128)} %fusion.223, bf16[2048,2048]{1,0:T(8,128)(2,1)} %all-gather.13.cloned.1.call-done, bf16[1024,1024]{1,0:T(8,128)(2,1)} %bitcast.430, ...), kind=kOutput, calls=%fused_computation.12 | convolution fusion | flops 8631877632 | bytes 41943040 | tf_op jit(solution)/shard_map/dot_general | solution.py:36
  435.1 11.0 %collective-permute-done.16 = bf16[512,1024]{1,0:T(8,128)(2,1)S(1)} collective-permute-done((bf16[512,1024]{1,0:T(8,128)(2,1)S(1)}, bf16[512,1024]{1,0:T(8,128)(2,1)S(1)}, u32[]{:S(2)}, u32[]{:S(2)}) %collective-permute-start.16) | collective-permute-done | bytes 1048608 | tf_op jit(solution)/shard_map/ppermute | solution.py:80
  456.6 10.8 %collective-permute-done.19 = bf16[256,1024]{1,0:T(8,128)(2,1)S(1)} collective-permute-done((bf16[256,1024]{1,0:T(8,128)(2,1)S(1)}, bf16[256,1024]{1,0:T(8,128)(2,1)S(1)}, u32[]{:S(2)}, u32[]{:S(2)}) %collective-permute-start.19) | collective-permute-done | bytes 524320 | tf_op jit(solution)/shard_map/ppermute | solution.py:85
  493.5 17.6 %collective-permute-done.23 = bf16[2,256,1024]{2,1,0:T(8,128)(2,1)S(1)} collective-permute-done((bf16[2,256,1024]{2,1,0:T(8,128)(2,1)S(1)}, bf16[2,256,1024]{2,1,0:T(8,128)(2,1)S(1)}, u32[]{:S(2)}, u32[]{:S(2)}) %collective-permute-start.23) | collective-permute-done | bytes 1048608 | tf_op jit(solution)/shard_map/ppermute | solution.py:109
  531.7 9.8 %fusion.115 = f32[1024,256]{0,1:T(8,128)} fusion(f32[1024,512,2]{1,0,2:T(8,128)} %fusion.188, f32[2,512,1024]{1,2,0:T(8,128)} %copy-done.21, f32[2,512]{1,0:T(2,128)S(1)} %log_add_fusion, f32[512,256]{0,1:T(8,128)} %fusion.125, bf16[1024,2,128]{0,2,1:T(8,128)(2,1)} %copy-done.44, bf16[1024,2,128]{0,2,1:T(8,128)(2,1)} %copy-done.42), kind=kOutput, calls=%fused_computation.153 | convolution fusion | flops 545523712 | bytes 11014144 | tf_op jit(solution)/shard_map/hqk,qhd->kd/dot_general | solution.py:161
  563.4 9.6 %fusion.113 = f32[512,2,256]{0,2,1:T(8,128)} fusion(f32[1024,512,2]{1,0,2:T(8,128)} %fusion.188, f32[2,512,1024]{1,2,0:T(8,128)} %copy-done.21, f32[2,512]{1,0:T(2,128)S(1)} %log_add_fusion, bf16[1024,128]{0,1:T(8,128)(2,1)} %copy-done.45, bf16[1024,128]{0,1:T(8,128)(2,1)} %copy-done.46), kind=kOutput, calls=%fused_computation.151 | convolution fusion | flops 545261568 | bytes 9965568 | tf_op jit(solution)/shard_map/hqk,kd->qhd/dot_general | solution.py:160
  579.9 14.1 %convolution_convert_fusion = bf16[2048,2048]{1,0:T(8,128)(2,1)} fusion(bf16[1024,2048]{1,0:T(8,128)(2,1)} %bitcast_multiply_fusion.1, bf16[1024,2048]{1,0:T(8,128)(2,1)} %get-tuple-element.117), kind=kOutput, calls=%fused_computation.15 | convolution fusion | flops 8594128896 | bytes 16777216 | tf_op jit(solution)/shard_map/dot_general | solution.py:44
  595.6 13.4 %convolution_convert_fusion.2 = bf16[2048,2048]{1,0:T(8,128)(2,1)} fusion(bf16[1024,2048]{1,0:T(8,128)(2,1)} %get-tuple-element.116, bf16[1024,1024]{1,0:T(8,128)(2,1)S(1)} %bitcast.431, bf16[1024,1024]{1,0:T(8,128)(2,1)} %bitcast.435), kind=kOutput, calls=%fused_computation.17 | convolution fusion | flops 8602517504 | bytes 16777216 | tf_op jit(solution)/shard_map/dot_general | solution.py:44
  609.1 13.6 %convolution_convert_fusion.1 = bf16[2048,2048]{1,0:T(8,128)(2,1)} fusion(bf16[1024,2048]{1,0:T(8,128)(2,1)} %get-tuple-element.118, bf16[1024,1024]{1,0:T(8,128)(2,1)S(1)} %bitcast.432, bf16[1024,1024]{1,0:T(8,128)(2,1)} %bitcast.436), kind=kOutput, calls=%fused_computation.16 | convolution fusion | flops 8602517504 | bytes 16777216 | tf_op jit(solution)/shard_map/dot_general | solution.py:44
  663.4 13.3 %collective-permute-done.26 = bf16[512,1024]{1,0:T(8,128)(2,1)S(1)} collective-permute-done((bf16[512,1024]{1,0:T(8,128)(2,1)S(1)}, bf16[512,1024]{1,0:T(8,128)(2,1)S(1)}, u32[]{:S(2)}, u32[]{:S(2)}) %collective-permute-start.26) | collective-permute-done | bytes 1048608 | tf_op jit(solution)/shard_map/ppermute | solution.py:81
  733.9 45.3 %psum.7 = f32[2,2048]{1,0:T(2,128)S(1)} all-reduce(f32[2,2048]{1,0:T(2,128)S(1)} %pad_maximum_fusion.33), channel_id=1, replica_groups=mesh['dp'=8,'mp'=4] {'dp','mp'}, use_global_device_ids=true, to_apply=%region_12.13 | all-reduce | flops 4096 | bytes 32768 | tf_op jit(solution)/shard_map/psum | solution.py:298
  809.8 31.0 %reduce-scatter.13.cloned.1.call-done = bf16[256,2048]{1,0:T(8,128)(2,1)} async-done(((bf16[2048,2048]{1,0:T(8,128)(2,1)}), bf16[256,2048]{1,0:T(8,128)(2,1)}) %reduce-scatter.13.cloned.1.call-update) | async-done | bytes 1048592 | tf_op jit(solution)/shard_map/reduce_scatter | solution.py:189
  843.6 87.3 %reduce-scatter.15.cloned.1.call-done = bf16[256,2048]{1,0:T(8,128)(2,1)} async-done(((bf16[2048,2048]{1,0:T(8,128)(2,1)}), bf16[256,2048]{1,0:T(8,128)(2,1)}) %reduce-scatter.15.cloned.1.call-update) | async-done | bytes 1048592 | tf_op jit(solution)/shard_map/reduce_scatter | solution.py:189
  (395 shorter events, 390.6 us)
Async XLA Ops:
  7.2 39.1 %all-gather.9.cloned.1.call-start = ((), (), s32[]{:S(2)}) async-start(), calls=%async_computation.11 | async-start | bytes 2359296 | tf_op jit(solution)/shard_map/all_gather | solution.py:185
  7.9 66.1 %all-gather.7.cloned.1.call-start = ((), (), s32[]{:S(2)}) async-start(), calls=%async_computation.10 | async-start | bytes 2359296 | tf_op jit(solution)/shard_map/all_gather | solution.py:185
  27.2 78.3 %all-gather.11.cloned.1.call-start = ((), (), s32[]{:S(2)}) async-start(), calls=%async_computation.12 | async-start | bytes 2359296 | tf_op jit(solution)/shard_map/all_gather | solution.py:185
  28.0 175.2 %all-gather.17.cloned.1.call-start = ((), (), s32[]{:S(2)}) async-start(), calls=%async_computation.15 | async-start | bytes 9437184 | tf_op jit(solution)/shard_map/all_gather | solution.py:185
  28.5 241.8 %all-gather.15.cloned.1.call-start = ((), (), s32[]{:S(2)}) async-start(), calls=%async_computation.14 | async-start | bytes 9437184 | tf_op jit(solution)/shard_map/all_gather | solution.py:185
  29.1 323.3 %all-gather.13.cloned.1.call-start = ((), (), s32[]{:S(2)}) async-start(), calls=%async_computation.13 | async-start | bytes 9437184 | tf_op jit(solution)/shard_map/all_gather | solution.py:185
  29.7 754.8 %reduce-scatter.9.cloned.1.call-start = ((), (), s32[]{:S(2)}) async-start(), calls=%async_computation.17 | async-start | bytes 2359296 | tf_op jit(solution)/shard_map/reduce_scatter | solution.py:189
  108.5 25.6 %collective-permute-start.2 = (bf16[512,1024]{1,0:T(8,128)(2,1)}, bf16[512,1024]{1,0:T(8,128)(2,1)}, u32[]{:S(2)}, u32[]{:S(2)}) collective-permute-start(bf16[512,1024]{1,0:T(8,128)(2,1)} %convolution_convert_fusion.5), channel_id=1, source_target_pairs={{0,2},{2,0},{1,3},{3,1},{4,6},{6,4},{5,7},{7,5},{8,10},{10,8},{9,1... | collective-permute-start | bytes 3145736 | tf_op jit(solution)/shard_map/ppermute | solution.py:81
  119.0 26.4 %collective-permute-start = (bf16[512,1024]{1,0:T(8,128)(2,1)}, bf16[512,1024]{1,0:T(8,128)(2,1)}, u32[]{:S(2)}, u32[]{:S(2)}) collective-permute-start(bf16[512,1024]{1,0:T(8,128)(2,1)} %convolution_convert_fusion.6), channel_id=1, source_target_pairs={{0,1},{1,0},{2,3},{3,2},{4,5},{5,4},{6,7},{7,6},{8,9},{9,8},{10,11... | collective-permute-start | bytes 3145736 | tf_op jit(solution)/shard_map/ppermute | solution.py:80
  380.5 41.3 %collective-permute-start.10 = (bf16[512,1024]{1,0:T(8,128)(2,1)}, bf16[512,1024]{1,0:T(8,128)(2,1)}, u32[]{:S(2)}, u32[]{:S(2)}) collective-permute-start(bf16[512,1024]{1,0:T(8,128)(2,1)} %fusion.92), channel_id=1, source_target_pairs={{0,2},{2,0},{1,3},{3,1},{4,6},{6,4},{5,7},{7,5},{8,10},{10,8},{9,1... | collective-permute-start | bytes 3145736 | tf_op jit(solution)/shard_map/ppermute | solution.py:81
  390.1 38.5 %collective-permute-start.18 = (bf16[512,1024]{1,0:T(8,128)(2,1)}, bf16[512,1024]{1,0:T(8,128)(2,1)}, u32[]{:S(2)}, u32[]{:S(2)}) collective-permute-start(bf16[512,1024]{1,0:T(8,128)(2,1)} %add_convert_fusion.2), channel_id=1, source_target_pairs={{0,2},{2,0},{1,3},{3,1},{4,6},{6,4},{5,7},{7,5},{8,10},{10,8},{9,1... | collective-permute-start | bytes 3145736 | tf_op jit(solution)/shard_map/ppermute | solution.py:81
  397.4 55.7 %collective-permute-start.8 = (bf16[512,1024]{1,0:T(8,128)(2,1)}, bf16[512,1024]{1,0:T(8,128)(2,1)S(1)}, u32[]{:S(2)}, u32[]{:S(2)}) collective-permute-start(bf16[512,1024]{1,0:T(8,128)(2,1)} %fusion.98), channel_id=1, source_target_pairs={{0,1},{1,0},{2,3},{3,2},{4,5},{5,4},{6,7},{7,6},{8,9},{9,8},{10,11... | collective-permute-start | bytes 3145736 | tf_op jit(solution)/shard_map/ppermute | solution.py:80
  410.8 35.4 %collective-permute-start.16 = (bf16[512,1024]{1,0:T(8,128)(2,1)S(1)}, bf16[512,1024]{1,0:T(8,128)(2,1)S(1)}, u32[]{:S(2)}, u32[]{:S(2)}) collective-permute-start(bf16[512,1024]{1,0:T(8,128)(2,1)S(1)} %add_convert_fusion.3), channel_id=1, source_target_pairs={{0,1},{1,0},{2,3},{3,2},{4,5},{5,4},{6,7},{7,6},{8,9},{9,8},{10,11... | collective-permute-start | bytes 3145736 | tf_op jit(solution)/shard_map/ppermute | solution.py:80
  425.5 42.9 %collective-permute-start.11 = (bf16[256,1024]{1,0:T(8,128)(2,1)S(1)}, bf16[256,1024]{1,0:T(8,128)(2,1)S(1)}, u32[]{:S(2)}, u32[]{:S(2)}) collective-permute-start(bf16[256,1024]{1,0:T(8,128)(2,1)S(1)} %fusion.172), channel_id=1, source_target_pairs={{0,1},{1,0},{2,3},{3,2},{4,5},{5,4},{6,7},{7,6},{8,9},{9,8},{10,11... | collective-permute-start | bytes 1572872 | tf_op jit(solution)/shard_map/ppermute | solution.py:85
  433.6 33.8 %collective-permute-start.19 = (bf16[256,1024]{1,0:T(8,128)(2,1)S(1)}, bf16[256,1024]{1,0:T(8,128)(2,1)S(1)}, u32[]{:S(2)}, u32[]{:S(2)}) collective-permute-start(bf16[256,1024]{1,0:T(8,128)(2,1)S(1)} %fusion.174), channel_id=1, source_target_pairs={{0,1},{1,0},{2,3},{3,2},{4,5},{5,4},{6,7},{7,6},{8,9},{9,8},{10,11... | collective-permute-start | bytes 1572872 | tf_op jit(solution)/shard_map/ppermute | solution.py:85
  552.5 248.2 %reduce-scatter.11.cloned.1.call-start = ((), (), s32[]{:S(2)}) async-start(), calls=%async_computation.18 | async-start | bytes 2359296 | tf_op jit(solution)/shard_map/reduce_scatter | solution.py:189
  559.7 243.1 %reduce-scatter.7.cloned.1.call-start = ((), (), s32[]{:S(2)}) async-start(), calls=%async_computation.16 | async-start | bytes 2359296 | tf_op jit(solution)/shard_map/reduce_scatter | solution.py:189
  579.8 226.7 %reduce-scatter.17.cloned.1.call-start = ((), (), s32[]{:S(2)}) async-start(), calls=%async_computation.21 | async-start | bytes 9437184 | tf_op jit(solution)/shard_map/reduce_scatter | solution.py:189
  594.0 246.8 %reduce-scatter.13.cloned.1.call-start = ((), (), s32[]{:S(2)}) async-start(), calls=%async_computation.19 | async-start | bytes 9437184 | tf_op jit(solution)/shard_map/reduce_scatter | solution.py:189
  609.0 321.8 %reduce-scatter.15.cloned.1.call-start = ((), (), s32[]{:S(2)}) async-start(), calls=%async_computation.20 | async-start | bytes 9437184 | tf_op jit(solution)/shard_map/reduce_scatter | solution.py:189
  687.6 27.2 %collective-permute-start.15 = (bf16[2,256,1024]{2,1,0:T(8,128)(2,1)S(1)}, bf16[2,256,1024]{2,1,0:T(8,128)(2,1)S(1)}, u32[]{:S(2)}, u32[]{:S(2)}) collective-permute-start(bf16[2,256,1024]{2,1,0:T(8,128)(2,1)S(1)} %pad_maximum_fusion.21), channel_id=1, source_target_pairs={{0,2},{2,0},{1,3},{3,1},{4,6},{6,4},{5,7},{7,5},{8,10},{10,8},{9,1... | collective-permute-start | bytes 3145736 | tf_op jit(solution)/shard_map/ppermute | solution.py:109
  689.1 28.8 %collective-permute-start.13 = (bf16[2,256,1024]{2,1,0:T(8,128)(2,1)S(1)}, bf16[2,256,1024]{2,1,0:T(8,128)(2,1)S(1)}, u32[]{:S(2)}, u32[]{:S(2)}) collective-permute-start(bf16[2,256,1024]{2,1,0:T(8,128)(2,1)S(1)} %pad_maximum_fusion.20), channel_id=1, source_target_pairs={{0,1},{1,0},{2,3},{3,2},{4,5},{5,4},{6,7},{7,6},{8,9},{9,8},{10,11... | collective-permute-start | bytes 3145736 | tf_op jit(solution)/shard_map/ppermute | solution.py:108
  727.7 52.1 %collective-permute-start.29 = (bf16[2,256,1024]{2,1,0:T(8,128)(2,1)}, bf16[2,256,1024]{2,1,0:T(8,128)(2,1)}, u32[]{:S(2)}, u32[]{:S(2)}) collective-permute-start(bf16[2,256,1024]{2,1,0:T(8,128)(2,1)} %pad_maximum_fusion.26), channel_id=1, source_target_pairs={{0,1},{1,0},{2,3},{3,2},{4,5},{5,4},{6,7},{7,6},{8,9},{9,8},{10,11... | collective-permute-start | bytes 3145736 | tf_op jit(solution)/shard_map/ppermute | solution.py:108
  730.9 50.8 %collective-permute-start.31 = (bf16[2,256,1024]{2,1,0:T(8,128)(2,1)}, bf16[2,256,1024]{2,1,0:T(8,128)(2,1)}, u32[]{:S(2)}, u32[]{:S(2)}) collective-permute-start(bf16[2,256,1024]{2,1,0:T(8,128)(2,1)} %pad_maximum_fusion.27), channel_id=1, source_target_pairs={{0,2},{2,0},{1,3},{3,1},{4,6},{6,4},{5,7},{7,5},{8,10},{10,8},{9,1... | collective-permute-start | bytes 3145736 | tf_op jit(solution)/shard_map/ppermute | solution.py:109
  (89 other events, 750.2 us)
Sparse Core Ops, SparseCore 0:
  9.6 31.8 all-gather.8
  43.6 30.3 all-gather.6
  75.6 29.8 all-gather.10
  107.0 81.5 all-gather.16
  190.1 80.2 all-gather.14
  271.8 80.5 all-gather.12
  552.7 33.2 reduce-scatter.8
  588.3 34.4 reduce-scatter.10
  625.1 34.3 reduce-scatter.6
  661.6 88.2 reduce-scatter.16
  752.2 88.5 reduce-scatter.12
  843.0 87.8 reduce-scatter.14
where the time goes:
time: 945 us; the launch traced here: 941 us
  waiting for transfers between devices  440 us (47%)
  matrix products  233 us (25%)
  blocking collectives  75.8 us (8%)
  local copies, waits for them, and re-layouts  65.4 us (7%)
  other arithmetic  63.3 us (7%)
  starting transfers between devices  47 us (5%)
  between operations  16.5 us (2%)
    all_gather x6, waiting for transfers between devices, gather_dp(): return lax.all_gather(block, 'dp', axis=0, tiled=True)  149 us
    reduce_scatter x6, waiting for transfers between devices, reduce_dp(): return lax.psum_scatter(block, 'dp', scatter_dimension=0, tiled=True)  118 us
    dot_general x24, matrix products, mm_t(): lax.dot_general(left, right, (((1,), (1,)), ((), ())), preferred_element_...  71.9 us
    dot_general x6, matrix products, mm(): lax.dot_general(left, right, (((1,), (0,)), ((), ())), preferred_element_...  64.1 us
    dot_general x6, matrix products, mm_rows(): lax.dot_general(left, right, (((0,), (0,)), ((), ())), preferred_element_...  57.4 us
    psum x1, blocking collectives, local(): lax.psum(jnp.stack([gain_attn_part, gain_ffn_part]), ('dp', 'mp'))  45.3 us
    ppermute x4, waiting for transfers between devices, gather_rows(): far_b = lax.ppermute(pair_b, 'mp', OVER_Y)  42.4 us
    unnamed x144, local copies, waits for them, and re-layouts  37.5 us
  transfers between devices with their start and end apart: 46, of which 32 were waited for; matrix products, arithmetic and copies ran while one was open for 29% of the time, Pallas kernels for 0%

commit v1 on v0

--- a/solution.py
+++ b/solution.py
@@ -11,6 +11,27 @@
 neg_large = -1e30
 bf16 = jnp.bfloat16
 f32 = jnp.float32
+
+
+def gather_around(x, axis, dim):
+    size, index, rows = (lax.axis_size(axis), lax.axis_index(axis), x.shape[dim])
+    right = [(i, (i + 1) % size) for i in range(size)]
+    downward = [(i, (i - 1) % size) for i in range(size)]
+    filled = jnp.zeros((*x.shape[:dim], size * rows, *x.shape[dim + 1 :]), x.dtype)
+    filled = lax.dynamic_update_slice_in_dim(filled, x, index * rows, axis=dim)
+    from_left = from_right = x
+    half = size // 2
+    for step in range(1, half + 1):
+        from_left = lax.ppermute(from_left, axis, right)
+        filled = lax.dynamic_update_slice_in_dim(
+            filled, from_left, (index - step) % size * rows, axis=dim
+        )
+        if step < size - half:
+            from_right = lax.ppermute(from_right, axis, downward)
+            filled = lax.dynamic_update_slice_in_dim(
+                filled, from_right, (index + step) % size * rows, axis=dim
+            )
+    return filled
 
 
 def rope_tables(slot_length, size):
@@ -182,7 +203,7 @@
 
 
 def gather_dp(block):
-    return lax.all_gather(block, "dp", axis=0, tiled=True)
+    return gather_around(block, "dp", 0)
 
 
 def reduce_dp(block):

time: 945 us -> 1010 us (1.069)
  waiting for transfers between devices: 440 us -> 314 us
  local copies, waits for them, and re-layouts: 65.4 us -> 172 us
  starting transfers between devices: 47 us -> 124 us
    all_gather x6 -> x0, waiting for transfers between devices: 149 us -> none  [gather_dp(): return lax.all_gather(block, 'dp', axis=0, tiled=True)]
    ppermute x0 -> x42, waiting for transfers between devices: none -> 93.4 us  [the longest x24 90.6 us: gather_around(): from_left = lax.ppermute(from_left, axis, right)]
    ppermute x0 -> x42, starting transfers between devices: none -> 74.6 us  [the longest x18 62.7 us: gather_around(): from_right = lax.ppermute(from_right, axis, downward)]
    dynamic_update_slice x0 -> x47, local copies, waits for them, and re-layouts: none -> 55.6 us  [the longest x24 27.2 us: gather_around(): lax.dynamic_update_slice_in_dim(filled, from_left, (index - step) % size...]
    ppermute x4, waiting for transfers between devices: 42.4 us -> 1.21 us  [gather_rows(): far_b = lax.ppermute(pair_b, 'mp', OVER_Y)]
    ppermute x0 -> x21, local copies, waits for them, and re-layouts: none -> 33.6 us  [the longest x12 18.3 us: gather_around(): from_left = lax.ppermute(from_left, axis, right)]
    ppermute x4, waiting for transfers between devices: 25.3 us -> 0.01 us  [scatter_rows(): away_a = lax.ppermute(product(rows_x(1 - x), 0).astype(bf16), 'mp', OVER_X)]
    ppermute x4, waiting for transfers between devices: 4.18 us -> 24.3 us  [gather_rows(): far_a = lax.ppermute(pair_a, 'mp', OVER_X)]
  transfers between devices with their start and end apart: 46 -> 84, of which waited for: 32 -> 24; matrix products, arithmetic and copies ran while one was open for 29% -> 37% of each run, Pallas kernels for 0% -> 0%
where the time goes in v1:
time: 1010 us; the launch traced here: 1000 us
  waiting for transfers between devices  314 us (31%)
  matrix products  232 us (23%)
  local copies, waits for them, and re-layouts  172 us (17%)
  starting transfers between devices  124 us (12%)
  other arithmetic  72.9 us (7%)
  blocking collectives  68.3 us (7%)
  between operations  17.1 us (2%)
    reduce_scatter x6, waiting for transfers between devices, reduce_dp(): return lax.psum_scatter(block, 'dp', scatter_dimension=0, tiled=True)  100 us
    ppermute x24, waiting for transfers between devices, gather_around(): from_left = lax.ppermute(from_left, axis, right)  90.6 us
    dot_general x24, matrix products, mm_t(): lax.dot_general(left, right, (((1,), (1,)), ((), ())), preferred_element_...  76.3 us
    ppermute x18, starting transfers between devices, gather_around(): from_right = lax.ppermute(from_right, axis, downward)  62.7 us
    psum x1, blocking collectives, local(): lax.psum(jnp.stack([gain_attn_part, gain_ffn_part]), ('dp', 'mp'))  59.9 us
    dot_general x6, matrix products, mm_rows(): lax.dot_general(left, right, (((0,), (0,)), ((), ())), preferred_element_...  56.7 us
    dot_general x6, matrix products, mm(): lax.dot_general(left, right, (((1,), (0,)), ((), ())), preferred_element_...  56.6 us
    unnamed x203, local copies, waits for them, and re-layouts  41.3 us
  transfers between devices with their start and end apart: 84, of which 24 were waited for; matrix products, arithmetic and copies ran while one was open for 37% of the time, Pallas kernels for 0%

profile of v1, /device:TPU:0, one launch (start us, length us, event | category | flops | bytes accessed | tf_op | source)
XLA Modules:
  0.0 999.8 jit_solution(5895622164575886406)
XLA Ops:
  21.9 8.4 all_gather.3
  123.3 39.4 %collective-permute-done.13 = bf16[256,512]{1,0:T(8,128)(2,1)S(1)} collective-permute-done((bf16[256,512]{1,0:T(8,128)(2,1)}, bf16[256,512]{1,0:T(8,128)(2,1)S(1)}, u32[]{:S(2)}, u32[]{:S(2)}) %collective-permute-start.13) | collective-permute-done | bytes 262176 | tf_op jit(solution)/shard_map/ppermute | solution.py:25
  163.6 6.6 fusion.12
  175.3 11.0 %collective-permute-start.20 = (bf16[256,512]{0,1:T(8,128)(2,1)}, bf16[256,512]{0,1:T(8,128)(2,1)}, u32[]{:S(2)}, u32[]{:S(2)}) collective-permute-start(bf16[256,512]{0,1:T(8,128)(2,1)} %copy-done.66), channel_id=1, source_target_pairs={{0,4},{4,8},{8,12},{12,16},{16,20},{20,24},{24,28},{28,0},{1,5},{5... | collective-permute-start | bytes 786440 | tf_op jit(solution)/shard_map/ppermute | solution.py:25
  304.9 33.8 %collective-permute-done.33 = bf16[256,2048]{1,0:T(8,128)(2,1)} collective-permute-done((bf16[256,2048]{1,0:T(8,128)(2,1)}, bf16[256,2048]{1,0:T(8,128)(2,1)}, u32[]{:S(2)}, u32[]{:S(2)}) %collective-permute-start.33) | collective-permute-done | bytes 1048608 | tf_op jit(solution)/shard_map/ppermute | solution.py:25
  358.7 17.3 %collective-permute-done.49 = bf16[256,2048]{0,1:T(8,128)(2,1)S(1)} collective-permute-done((bf16[256,2048]{0,1:T(8,128)(2,1)}, bf16[256,2048]{0,1:T(8,128)(2,1)S(1)}, u32[]{:S(2)}, u32[]{:S(2)}) %collective-permute-start.49) | collective-permute-done | bytes 1048608 | tf_op jit(solution)/shard_map/ppermute | solution.py:25
  376.2 11.2 %fusion.229 = f32[1024,2048]{1,0:T(8,128)} fusion(bf16[1024,2048]{1,0:T(8,128)(2,1)S(1)} %copy-done.16, bf16[2048,2048]{0,1:T(8,128)(2,1)S(1)} %constant_dynamic-update-slice_fusion), kind=kOutput, calls=%fused_computation.413 | convolution fusion | flops 8589934592 | bytes 20971520 | tf_op jit(solution)/shard_map/dot_general | solution.py:57
  400.7 11.0 %fusion.215 = f32[1024,2048]{1,0:T(8,128)} fusion(bf16[2048,2048]{0,1:T(8,128)(2,1)S(1)} %bitcast.394, bf16[1024,1024]{1,0:T(8,128)(2,1)S(1)} %bitcast.443, bf16[1024,1024]{1,0:T(8,128)(2,1)S(1)} %bitcast.439), kind=kOutput, calls=%fused_computation.399 | convolution fusion | flops 8598323200 | bytes 20971520 | tf_op jit(solution)/shard_map/dot_general | solution.py:57
  411.7 21.2 %multiply_convert_fusion.1 = (bf16[1024,2048]{1,0:T(8,128)(2,1)}, bf16[1024,2048]{1,0:T(8,128)(2,1)}, bf16[1024,2048]{1,0:T(8,128)(2,1)}) fusion(f32[1024,2048]{1,0:T(8,128)} %fusion.229, f32[1024,2048]{1,0:T(8,128)} %fusion.215, bf16[2048,2048]{0,1:T(8,128)(2,1)} %constant_dynamic-update-slice_fusion.16, bf16[1024,1024]{1,0:T(8,128)(2,1)} %bitcast.444, ...), kind=kOutput, calls=%fused_computation.12 | convolution fusion | flops 8631877632 | bytes 41943040 | tf_op jit(solution)/shard_map/dot_general | solution.py:57
  494.7 16.0 %collective-permute-done.60 = bf16[512,1024]{1,0:T(8,128)(2,1)S(1)} collective-permute-done((bf16[512,1024]{1,0:T(8,128)(2,1)S(1)}, bf16[512,1024]{1,0:T(8,128)(2,1)S(1)}, u32[]{:S(2)}, u32[]{:S(2)}) %collective-permute-start.60) | collective-permute-done | bytes 1048608 | tf_op jit(solution)/shard_map/ppermute | solution.py:102
  516.1 11.1 %collective-permute-done.59 = bf16[256,1024]{1,0:T(8,128)(2,1)S(1)} collective-permute-done((bf16[256,1024]{1,0:T(8,128)(2,1)S(1)}, bf16[256,1024]{1,0:T(8,128)(2,1)S(1)}, u32[]{:S(2)}, u32[]{:S(2)}) %collective-permute-start.59) | collective-permute-done | bytes 524320 | tf_op jit(solution)/shard_map/ppermute | solution.py:105
  537.3 11.8 %collective-permute-done.62 = bf16[256,1024]{1,0:T(8,128)(2,1)S(1)} collective-permute-done((bf16[256,1024]{1,0:T(8,128)(2,1)S(1)}, bf16[256,1024]{1,0:T(8,128)(2,1)S(1)}, u32[]{:S(2)}, u32[]{:S(2)}) %collective-permute-start.62) | collective-permute-done | bytes 524320 | tf_op jit(solution)/shard_map/ppermute | solution.py:125
  552.2 12.0 %collective-permute-done.63 = bf16[2,256,1024]{2,1,0:T(8,128)(2,1)S(1)} collective-permute-done((bf16[2,256,1024]{2,1,0:T(8,128)(2,1)S(1)}, bf16[2,256,1024]{2,1,0:T(8,128)(2,1)S(1)}, u32[]{:S(2)}, u32[]{:S(2)}) %collective-permute-start.63) | collective-permute-done | bytes 1048608 | tf_op jit(solution)/shard_map/ppermute | solution.py:129
  584.6 8.7 fusion.111
  618.1 9.4 fusion.109
  635.0 14.1 %convolution_convert_fusion = bf16[2048,2048]{1,0:T(8,128)(2,1)} fusion(bf16[1024,2048]{1,0:T(8,128)(2,1)} %bitcast_multiply_fusion.1, bf16[1024,2048]{1,0:T(8,128)(2,1)} %get-tuple-element.117), kind=kOutput, calls=%fused_computation.15 | convolution fusion | flops 8594128896 | bytes 16777216 | tf_op jit(solution)/shard_map/dot_general | solution.py:65
  649.6 14.2 %convolution_convert_fusion.1 = bf16[2048,2048]{1,0:T(8,128)(2,1)} fusion(bf16[1024,2048]{1,0:T(8,128)(2,1)} %get-tuple-element.118, bf16[1024,1024]{1,0:T(8,128)(2,1)} %bitcast.445, bf16[1024,1024]{1,0:T(8,128)(2,1)} %bitcast.441), kind=kOutput, calls=%fused_computation.16 | convolution fusion | flops 8602517504 | bytes 16777216 | tf_op jit(solution)/shard_map/dot_general | solution.py:65
  663.9 14.2 %convolution_convert_fusion.2 = bf16[2048,2048]{1,0:T(8,128)(2,1)} fusion(bf16[1024,2048]{1,0:T(8,128)(2,1)} %get-tuple-element.116, bf16[1024,1024]{1,0:T(8,128)(2,1)} %bitcast.446, bf16[1024,1024]{1,0:T(8,128)(2,1)} %bitcast.442), kind=kOutput, calls=%fused_computation.17 | convolution fusion | flops 8602517504 | bytes 16777216 | tf_op jit(solution)/shard_map/dot_general | solution.py:65
  733.5 16.6 %collective-permute-done.68 = bf16[512,1024]{1,0:T(8,128)(2,1)S(1)} collective-permute-done((bf16[512,1024]{1,0:T(8,128)(2,1)}, bf16[512,1024]{1,0:T(8,128)(2,1)S(1)}, u32[]{:S(2)}, u32[]{:S(2)}) %collective-permute-start.68) | collective-permute-done | bytes 1048608 | tf_op jit(solution)/shard_map/ppermute | solution.py:102
  766.2 12.3 %collective-permute-done.55 = bf16[2,256,1024]{2,1,0:T(8,128)(2,1)} collective-permute-done((bf16[2,256,1024]{2,1,0:T(8,128)(2,1)}, bf16[2,256,1024]{2,1,0:T(8,128)(2,1)}, u32[]{:S(2)}, u32[]{:S(2)}) %collective-permute-start.55) | collective-permute-done | bytes 1048608 | tf_op jit(solution)/shard_map/ppermute | solution.py:129
  780.3 7.8 collective-permute-done.70
  797.5 59.9 %psum.7 = f32[2,2048]{1,0:T(2,128)S(1)} all-reduce(f32[2,2048]{1,0:T(2,128)S(1)} %pad_maximum_fusion.33), channel_id=1, replica_groups=mesh['dp'=8,'mp'=4] {'dp','mp'}, use_global_device_ids=true, to_apply=%region_12.13 | all-reduce | flops 4096 | bytes 32768 | tf_op jit(solution)/shard_map/psum | solution.py:319
  886.7 13.1 %reduce-scatter.15.cloned.1.call-done = bf16[256,2048]{1,0:T(8,128)(2,1)} async-done(((bf16[2048,2048]{1,0:T(8,128)(2,1)}), bf16[256,2048]{1,0:T(8,128)(2,1)}) %reduce-scatter.15.cloned.1.call-update) | async-done | bytes 1048592 | tf_op jit(solution)/shard_map/reduce_scatter | solution.py:210
  902.6 87.3 %reduce-scatter.13.cloned.1.call-done = bf16[256,2048]{1,0:T(8,128)(2,1)} async-done(((bf16[2048,2048]{1,0:T(8,128)(2,1)}), bf16[256,2048]{1,0:T(8,128)(2,1)}) %reduce-scatter.13.cloned.1.call-update) | async-done | bytes 1048592 | tf_op jit(solution)/shard_map/reduce_scatter | solution.py:210
  (599 shorter events, 513.9 us)
Async XLA Ops:
  7.2 61.3 %collective-permute-start.7 = (bf16[256,512]{1,0:T(8,128)(2,1)}, bf16[256,512]{1,0:T(8,128)(2,1)}, u32[]{:S(2)}, u32[]{:S(2)}) collective-permute-start(bf16[256,512]{1,0:T(8,128)(2,1)} %param.27), channel_id=1, source_target_pairs={{0,4},{4,8},{8,12},{12,16},{16,20},{20,24},{24,28},{28,0},{1,5},{5... | collective-permute-start | bytes 786440 | tf_op jit(solution)/shard_map/ppermute | solution.py:25
  7.7 66.1 %collective-permute-start.8 = (bf16[256,512]{1,0:T(8,128)(2,1)}, bf16[256,512]{1,0:T(8,128)(2,1)}, u32[]{:S(2)}, u32[]{:S(2)}) collective-permute-start(bf16[256,512]{1,0:T(8,128)(2,1)} %param.27), channel_id=1, source_target_pairs={{0,28},{4,0},{8,4},{12,8},{16,12},{20,16},{24,20},{28,24},{1,29},{... | collective-permute-start | bytes 786440 | tf_op jit(solution)/shard_map/ppermute | solution.py:30
  11.8 63.8 %collective-permute-start.14 = (bf16[256,512]{0,1:T(8,128)(2,1)}, bf16[256,512]{0,1:T(8,128)(2,1)}, u32[]{:S(2)}, u32[]{:S(2)}) collective-permute-start(bf16[256,512]{0,1:T(8,128)(2,1)} %bitcast.464), channel_id=1, source_target_pairs={{0,4},{4,8},{8,12},{12,16},{16,20},{20,24},{24,28},{28,0},{1,5},{5... | collective-permute-start | bytes 786440 | tf_op jit(solution)/shard_map/ppermute | solution.py:25
  11.8 69.0 %collective-permute-start.15 = (bf16[256,512]{0,1:T(8,128)(2,1)}, bf16[256,512]{0,1:T(8,128)(2,1)}, u32[]{:S(2)}, u32[]{:S(2)}) collective-permute-start(bf16[256,512]{0,1:T(8,128)(2,1)} %bitcast.465), channel_id=1, source_target_pairs={{0,28},{4,0},{8,4},{12,8},{16,12},{20,16},{24,20},{28,24},{1,29},{... | collective-permute-start | bytes 786440 | tf_op jit(solution)/shard_map/ppermute | solution.py:30
  63.1 798.4 %reduce-scatter.9.cloned.1.call-start = ((), (), s32[]{:S(2)}) async-start(), calls=%async_computation.11 | async-start | bytes 2359296 | tf_op jit(solution)/shard_map/reduce_scatter | solution.py:210
  111.0 59.2 %collective-permute-start.36 = (bf16[256,2048]{1,0:T(8,128)(2,1)}, bf16[256,2048]{1,0:T(8,128)(2,1)}, u32[]{:S(2)}, u32[]{:S(2)}) collective-permute-start(bf16[256,2048]{1,0:T(8,128)(2,1)} %param.33), channel_id=1, source_target_pairs={{0,4},{4,8},{8,12},{12,16},{16,20},{20,24},{24,28},{28,0},{1,5},{5... | collective-permute-start | bytes 3145736 | tf_op jit(solution)/shard_map/ppermute | solution.py:25
  112.8 62.4 %collective-permute-start.37 = (bf16[256,2048]{1,0:T(8,128)(2,1)}, bf16[256,2048]{1,0:T(8,128)(2,1)}, u32[]{:S(2)}, u32[]{:S(2)}) collective-permute-start(bf16[256,2048]{1,0:T(8,128)(2,1)} %param.33), channel_id=1, source_target_pairs={{0,28},{4,0},{8,4},{12,8},{16,12},{20,16},{24,20},{28,24},{1,29},{... | collective-permute-start | bytes 3145736 | tf_op jit(solution)/shard_map/ppermute | solution.py:30
  117.1 71.5 %collective-permute-start.29 = (bf16[256,2048]{1,0:T(8,128)(2,1)}, bf16[256,2048]{1,0:T(8,128)(2,1)}, u32[]{:S(2)}, u32[]{:S(2)}) collective-permute-start(bf16[256,2048]{1,0:T(8,128)(2,1)} %param.32), channel_id=1, source_target_pairs={{0,4},{4,8},{8,12},{12,16},{16,20},{20,24},{24,28},{28,0},{1,5},{5... | collective-permute-start | bytes 3145736 | tf_op jit(solution)/shard_map/ppermute | solution.py:25
  117.1 73.8 %collective-permute-start.30 = (bf16[256,2048]{1,0:T(8,128)(2,1)}, bf16[256,2048]{1,0:T(8,128)(2,1)}, u32[]{:S(2)}, u32[]{:S(2)}) collective-permute-start(bf16[256,2048]{1,0:T(8,128)(2,1)} %param.32), channel_id=1, source_target_pairs={{0,28},{4,0},{8,4},{12,8},{16,12},{20,16},{24,20},{28,24},{1,29},{... | collective-permute-start | bytes 3145736 | tf_op jit(solution)/shard_map/ppermute | solution.py:30
  198.2 51.1 %collective-permute-start.39 = (bf16[256,2048]{1,0:T(8,128)(2,1)}, bf16[256,2048]{1,0:T(8,128)(2,1)}, u32[]{:S(2)}, u32[]{:S(2)}) collective-permute-start(bf16[256,2048]{1,0:T(8,128)(2,1)} %collective-permute-done.37), channel_id=1, source_target_pairs={{0,28},{4,0},{8,4},{12,8},{16,12},{20,16},{24,20},{28,24},{1,29},{... | collective-permute-start | bytes 3145736 | tf_op jit(solution)/shard_map/ppermute | solution.py:30
  205.9 52.2 %collective-permute-start.32 = (bf16[256,2048]{1,0:T(8,128)(2,1)}, bf16[256,2048]{1,0:T(8,128)(2,1)}, u32[]{:S(2)}, u32[]{:S(2)}) collective-permute-start(bf16[256,2048]{1,0:T(8,128)(2,1)} %collective-permute-done.30), channel_id=1, source_target_pairs={{0,28},{4,0},{8,4},{12,8},{16,12},{20,16},{24,20},{28,24},{1,29},{... | collective-permute-start | bytes 3145736 | tf_op jit(solution)/shard_map/ppermute | solution.py:30
  279.7 68.9 %collective-permute-start.47 = (bf16[256,2048]{0,1:T(8,128)(2,1)}, bf16[256,2048]{0,1:T(8,128)(2,1)}, u32[]{:S(2)}, u32[]{:S(2)}) collective-permute-start(bf16[256,2048]{0,1:T(8,128)(2,1)} %collective-permute-done.45), channel_id=1, source_target_pairs={{0,4},{4,8},{8,12},{12,16},{16,20},{20,24},{24,28},{28,0},{1,5},{5... | collective-permute-start | bytes 3145736 | tf_op jit(solution)/shard_map/ppermute | solution.py:25
  282.5 56.2 %collective-permute-start.33 = (bf16[256,2048]{1,0:T(8,128)(2,1)}, bf16[256,2048]{1,0:T(8,128)(2,1)}, u32[]{:S(2)}, u32[]{:S(2)}) collective-permute-start(bf16[256,2048]{1,0:T(8,128)(2,1)} %collective-permute-done.31), channel_id=1, source_target_pairs={{0,4},{4,8},{8,12},{12,16},{16,20},{20,24},{24,28},{28,0},{1,5},{5... | collective-permute-start | bytes 3145736 | tf_op jit(solution)/shard_map/ppermute | solution.py:25
  284.9 56.7 %collective-permute-start.34 = (bf16[256,2048]{1,0:T(8,128)(2,1)}, bf16[256,2048]{1,0:T(8,128)(2,1)}, u32[]{:S(2)}, u32[]{:S(2)}) collective-permute-start(bf16[256,2048]{1,0:T(8,128)(2,1)} %collective-permute-done.32), channel_id=1, source_target_pairs={{0,28},{4,0},{8,4},{12,8},{16,12},{20,16},{24,20},{28,24},{1,29},{... | collective-permute-start | bytes 3145736 | tf_op jit(solution)/shard_map/ppermute | solution.py:30
  293.8 57.4 %collective-permute-start.48 = (bf16[256,2048]{0,1:T(8,128)(2,1)}, bf16[256,2048]{0,1:T(8,128)(2,1)}, u32[]{:S(2)}, u32[]{:S(2)}) collective-permute-start(bf16[256,2048]{0,1:T(8,128)(2,1)} %collective-permute-done.46), channel_id=1, source_target_pairs={{0,28},{4,0},{8,4},{12,8},{16,12},{20,16},{24,20},{28,24},{1,29},{... | collective-permute-start | bytes 3145736 | tf_op jit(solution)/shard_map/ppermute | solution.py:30
  301.0 52.5 %collective-permute-start.25 = (bf16[256,1024]{1,0:T(8,128)(2,1)}, bf16[256,1024]{1,0:T(8,128)(2,1)}, u32[]{:S(2)}, u32[]{:S(2)}) collective-permute-start(bf16[256,1024]{1,0:T(8,128)(2,1)} %get-tuple-element.188), channel_id=1, source_target_pairs={{0,2},{2,0},{1,3},{3,1},{4,6},{6,4},{5,7},{7,5},{8,10},{10,8},{9,1... | collective-permute-start | bytes 1572872 | tf_op jit(solution)/shard_map/ppermute | solution.py:125
  453.2 59.3 %collective-permute-start.52 = (bf16[512,1024]{1,0:T(8,128)(2,1)}, bf16[512,1024]{1,0:T(8,128)(2,1)S(1)}, u32[]{:S(2)}, u32[]{:S(2)}) collective-permute-start(bf16[512,1024]{1,0:T(8,128)(2,1)} %fusion.92), channel_id=1, source_target_pairs={{0,2},{2,0},{1,3},{3,1},{4,6},{6,4},{5,7},{7,5},{8,10},{10,8},{9,1... | collective-permute-start | bytes 3145736 | tf_op jit(solution)/shard_map/ppermute | solution.py:102
  604.1 273.6 %reduce-scatter.11.cloned.1.call-start = ((), (), s32[]{:S(2)}) async-start(), calls=%async_computation.12 | async-start | bytes 2359296 | tf_op jit(solution)/shard_map/reduce_scatter | solution.py:210
  611.3 268.4 %reduce-scatter.7.cloned.1.call-start = ((), (), s32[]{:S(2)}) async-start(), calls=%async_computation.10 | async-start | bytes 2359296 | tf_op jit(solution)/shard_map/reduce_scatter | solution.py:210
  635.0 248.5 %reduce-scatter.17.cloned.1.call-start = ((), (), s32[]{:S(2)}) async-start(), calls=%async_computation.15 | async-start | bytes 9437184 | tf_op jit(solution)/shard_map/reduce_scatter | solution.py:210
  649.2 250.6 %reduce-scatter.15.cloned.1.call-start = ((), (), s32[]{:S(2)}) async-start(), calls=%async_computation.14 | async-start | bytes 9437184 | tf_op jit(solution)/shard_map/reduce_scatter | solution.py:210
  663.9 326.1 %reduce-scatter.13.cloned.1.call-start = ((), (), s32[]{:S(2)}) async-start(), calls=%async_computation.13 | async-start | bytes 9437184 | tf_op jit(solution)/shard_map/reduce_scatter | solution.py:210
  790.9 67.1 %collective-permute-start.71 = (bf16[2,256,1024]{2,1,0:T(8,128)(2,1)}, bf16[2,256,1024]{2,1,0:T(8,128)(2,1)S(1)}, u32[]{:S(2)}, u32[]{:S(2)}) collective-permute-start(bf16[2,256,1024]{2,1,0:T(8,128)(2,1)} %pad_maximum_fusion.26), channel_id=1, source_target_pairs={{0,1},{1,0},{2,3},{3,2},{4,5},{5,4},{6,7},{7,6},{8,9},{9,8},{10,11... | collective-permute-start | bytes 3145736 | tf_op jit(solution)/shard_map/ppermute | solution.py:129
  794.0 64.6 %collective-permute-start.73 = (bf16[2,256,1024]{2,1,0:T(8,128)(2,1)}, bf16[2,256,1024]{2,1,0:T(8,128)(2,1)}, u32[]{:S(2)}, u32[]{:S(2)}) collective-permute-start(bf16[2,256,1024]{2,1,0:T(8,128)(2,1)} %pad_maximum_fusion.27), channel_id=1, source_target_pairs={{0,2},{2,0},{1,3},{3,1},{4,6},{6,4},{5,7},{7,5},{8,10},{10,8},{9,1... | collective-permute-start | bytes 3145736 | tf_op jit(solution)/shard_map/ppermute | solution.py:130
  (155 other events, 2364.5 us)
Sparse Core Ops, SparseCore 0:
  604.3 40.3 reduce-scatter.8
  646.9 34.4 reduce-scatter.10
  683.7 34.4 reduce-scatter.6
  720.3 88.2 reduce-scatter.16
  810.8 89.0 reduce-scatter.14
  902.0 87.9 reduce-scatter.12
